TPU v7x, 32 devices: a whole 2x2x4 slice. The times are simulated.
32 devices in a mesh: seq: 2 (over x), exp: 16 (over z, y, core).
Axes of the slice: x: 2, y: 2, z: 4, core: 2. Of those that a mesh axis runs over, the one named last changes fastest.
Arguments:
- queries: bfloat16 [2048, 64, 576], P('seq', 'exp'), may hold values from -68 to 68
- keys: bfloat16 [2048, 576], P(('seq', 'exp')), may hold values from -4.5 to 4.5
- block_mask: int32 [4, 4, 8], replicated, may hold values from 0 to 1, as said below
- summary_start: int32 [4], replicated, may hold values from 0 to 448, as said below
Outputs:
- context: bfloat16 [2048, 64, 512], P('seq', 'exp')
Inputs may be any that keep to these rules, and one draw needn't show every extreme that they name: block_mask[c, i, i] is 1, entries of own blocks j > i are 0, and entry 4 + c (the candidate's own summary) is 0. `summary_start`: every value is a multiple of 64.
All inputs are finite; a program needn't handle non-finite values.
Results may differ from a plain program's by a relative error of at most 0.0035.
Values may be sent and summed in bfloat16 or wider, within the bound.
No kernel may reach another device: no remote copies, remote signals or barrier semaphores. Data moves between devices by JAX's collectives and lax.ppermute only.
A program may use at most 64 MiB of HBM per device.

v0:
```python
import functools
import itertools
import math

import jax
import jax.numpy as jnp
from jax import lax
from jax.experimental import pallas as pl
from jax.experimental.pallas import tpu as pltpu
from jax.sharding import PartitionSpec as P

ROPE = 64
NBLK = 4
TILE = 256
MOST_BODIES = 9

score_scale = 192.0 ** (-0.5) * math.log2(math.e)
neg_big = -1e30


def step_orders(count):
    bits = [1 << k for k in range(1, count.bit_length() - 1)]
    bits.reverse()
    first = bits[:1] + bits[:0:-1]
    return first, first[-1:] + first[:-1]


def slot_offsets(order):
    offsets = [0]
    for bit in order:
        offsets = offsets + [o ^ bit for o in offsets]
    return offsets


def grant(mib):
    return pltpu.CompilerParams(vmem_limit_bytes=mib << 20)


def join_kernel(first_ref, second_ref, out_ref):
    half = first_ref.shape[0]
    out_ref[:half] = first_ref[...]
    out_ref[half:] = second_ref[...]


def join(first, second):
    vmem = pl.BlockSpec(memory_space=pltpu.VMEM)
    return pl.pallas_call(
        join_kernel,
        out_shape=jax.ShapeDtypeStruct((2 * first.shape[0],) + first.shape[1:], first.dtype),
        in_specs=[vmem, vmem],
        out_specs=vmem,
        compiler_params=grant(2),
        name="join",
    )(first, second)


def keep_kernel(in_ref, out_ref):
    out_ref[...] = in_ref[...]


def keep(array):
    vmem = pl.BlockSpec(memory_space=pltpu.VMEM)
    return pl.pallas_call(
        keep_kernel,
        out_shape=jax.ShapeDtypeStruct(array.shape, array.dtype),
        in_specs=[vmem],
        out_specs=vmem,
        compiler_params=grant(2),
        name="keep",
    )(array)


def turn_kernel(in_ref, out_ref):
    for h in range(in_ref.shape[0]):
        out_ref[h] = in_ref[h].T


def turn(by_width, head, total):
    _, width, rows = by_width.shape
    cut = min(rows, 256)
    return pl.pallas_call(
        turn_kernel,
        out_shape=jax.ShapeDtypeStruct((total, rows, width), by_width.dtype),
        grid=(total, rows // cut),
        in_specs=[pl.BlockSpec((1, width, cut), lambda h, i: (head + h, 0, i))],
        out_specs=pl.BlockSpec((1, cut, width), lambda h, i: (h, i, 0)),
        compiler_params=grant(4),
        name="turn",
    )(by_width)


def gather_steps(keys, queries):
    count = lax.axis_size("exp")
    heads = queries.shape[1]
    first, second = step_orders(count)
    last = len(first)
    by_width = jnp.transpose(queries, (1, 2, 0))
    swap = [(i, i ^ 1) for i in range(count)]
    by_head = []
    done = 0
    held = keys[None]
    for k, (bit_a, bit_b) in enumerate(zip(first, second)):
        pairs = [(i, i ^ (bit_b if i & 1 else bit_a)) for i in range(count)]
        got = lax.ppermute(held, "exp", pairs)
        if k == 0:
            got, held = lax.optimization_barrier((got, keep(held)))
        due = heads if k == last - 1 else heads * k // (2 * (last - 1))
        if k == last - 1:
            other = lax.ppermute(held, "exp", swap)
            got, other = lax.optimization_barrier((got, other))
        if due > done:
            piece = turn(by_width, done, due - done)
            got, piece = lax.optimization_barrier((got, piece))
            by_head.append(piece)
            done = due
        if k < last - 1:
            held = join(held, got)
    return (held, got), (other, lax.ppermute(got, "exp", swap)), by_head


def pick_kernel(cpg, orders, start_ref, *refs):
    buffers, own_ref = refs[:-1], refs[-1]
    me = lax.axis_index("exp")
    group = lax.axis_index("seq")
    half, shard, _ = buffers[0].shape
    summ = own_ref.shape[0] // cpg
    length = 4 * half * shard // cpg
    piece = min(shard, summ)
    starts = start_ref[...].astype(jnp.float32)
    cands = lax.broadcasted_iota(jnp.int32, starts.shape, 1)
    for member in range(cpg):
        start = jnp.sum(jnp.where(cands == group * cpg + member, starts, 0.0)).astype(jnp.int32)
        for k in range(summ // piece):
            row = member * length + start + k * piece
            owner = row // shard
            inside = pl.multiple_of(lax.rem(row, shard), piece)
            slots = [
                sum(((owner ^ me) // bit % 2) << place for place, bit in enumerate(order))
                for order in orders
            ]
            part = owner % 2
            slot = jnp.where(part == 0, slots[0], slots[1])
            buffer = jnp.where(part == me % 2, 0, 2) + slot // half
            at = slice(member * summ + k * piece, member * summ + (k + 1) * piece)
            for number, ref in enumerate(buffers):

                @pl.when(buffer == number)
                def _():
                    own_ref[at, :] = ref[lax.rem(slot, half), pl.ds(inside, piece), :]


def order_kernel(offsets_a, offsets_b, *refs):
    buffers, keys_ref = refs[:-1], refs[-1]
    me = lax.axis_index("exp")
    part = me % 2
    half, shard, _ = buffers[0].shape
    for s, (a, b) in enumerate(zip(offsets_a, offsets_b)):
        here = (me ^ jnp.where(part == 0, a, b)) * shard
        there = (me ^ 1 ^ jnp.where(part == 0, b, a)) * shard
        for target, ref in ((here, buffers[s // half]), (there, buffers[2 + s // half])):
            keys_ref[pl.ds(pl.multiple_of(target, shard), shard), :] = ref[s % half]


def prepare_kernel(dims, mask_ref, keys_ref, own_ref, near_ref):
    heads, cpg, cands, length, block, summ, lat = dims
    group = lax.axis_index("seq")
    tail = (cands - cpg) * summ + TILE

    def step(i, _):
        member, b = i // NBLK, lax.rem(i, NBLK)
        cand = group * cpg + member
        near_ref[i, 0:block, :] = keys_ref[pl.ds(pl.multiple_of(i * block, block), block), :]
        n = jnp.int32(block)
        for j in range(NBLK - 1):
            seen = jnp.logical_and(j < b, mask_ref[cand, b, j] == 1)

            @pl.when(seen)
            def _():
                near_ref[i, pl.ds(pl.multiple_of(n, summ), block), :] = keys_ref[
                    pl.ds(pl.multiple_of(member * length + j * block, block), block), :
                ]

            n = n + jnp.where(seen, block, 0)
        for d in range(cpg):
            seen = mask_ref[cand, b, NBLK + group * cpg + d] == 1

            @pl.when(seen)
            def _():
                near_ref[i, pl.ds(pl.multiple_of(n, summ), summ), :] = own_ref[
                    d * summ : (d + 1) * summ, :
                ]

            n = n + jnp.where(seen, summ, 0)
        near_ref[i, pl.ds(pl.multiple_of(n, summ), tail), :] = jnp.zeros(
            (tail, near_ref.shape[2]), near_ref.dtype
        )
        return 0

    lax.fori_loop(0, cpg * NBLK, step, 0)


def attend_kernel(dims, most, mask_ref, got_ref, sums_ref, *refs):
    heads, cpg, cands, length, block, summ, lat = dims
    q_refs, (out_ref, near, total_ref, part_ref, staged, sem) = refs[:-6], refs[-6:]
    group = lax.axis_index("seq")
    rows = heads * block

    def out_copy(b, member, slot):
        at = pl.ds(pl.multiple_of(member * length + b * block, block), block)
        return pltpu.make_async_copy(
            staged.at[slot, member], out_ref.at[at], sem.at[slot, member]
        )

    def put(slot):
        for member in range(cpg):
            result = (total_ref[member] * part_ref[member]).astype(jnp.bfloat16)
            staged[slot, member] = jnp.swapaxes(result.reshape(heads, block, lat), 0, 1)

    def add_seen(b, member):
        cand = group * cpg + member
        n = jnp.int32(block)
        for j in range(NBLK - 1):
            n = n + jnp.where(jnp.logical_and(j < b, mask_ref[cand, b, j] == 1), block, 0)
        for d in range(cpg):
            n = n + jnp.where(mask_ref[cand, b, NBLK + group * cpg + d] == 1, summ, 0)
        for d in range(cands):
            seen = jnp.logical_and(mask_ref[cand, b, NBLK + d] == 1, d // cpg != group)
            row = ((group ^ (d // cpg)) * cpg + d % cpg) * summ

            @pl.when(seen)
            def _():
                near[member * NBLK + b, pl.ds(pl.multiple_of(n, summ), summ), :] = sums_ref[
                    pl.ds(pl.multiple_of(row, summ), summ), :
                ]

            n = n + jnp.where(seen, summ, 0)
        return n

    def step(b, _):
        slot = lax.rem(b + 1, 2)
        counts = [add_seen(b, member) for member in range(cpg)]

        @pl.when(b >= 3)
        def _():
            for member in range(cpg):
                out_copy(b - 3, member, slot).wait()

        def attend(totals):
            put(slot)
            all_scores = []
            for member, total in enumerate(totals):
                at = pl.ds(pl.multiple_of(member * length + b * block, block), block)
                q = jnp.concatenate(
                    [q_ref[h, at, :] for q_ref in q_refs for h in range(q_ref.shape[0])], axis=0
                )
                all_scores.append(
                    lax.dot_general(
                        q,
                        near[member * NBLK + b, :total, :],
                        (((1,), (1,)), ((), ())),
                        preferred_element_type=jnp.float32,
                    )
                )
            pos = lax.rem(lax.broadcasted_iota(jnp.int32, (rows, block), 0), block)
            causal = lax.broadcasted_iota(jnp.int32, (rows, block), 1) <= pos
            for member, (total, scores) in enumerate(zip(totals, all_scores)):
                col = lax.broadcasted_iota(jnp.int32, (1, total - block), 1) + block
                bias = jnp.where(col < counts[member], 0.0, neg_big)
                first = jnp.where(causal, scores[:, :block] * score_scale, neg_big)
                rest = scores[:, block:] * score_scale + bias
                most_score = jnp.maximum(
                    jnp.max(first, axis=1, keepdims=True), jnp.max(rest, axis=1, keepdims=True)
                )
                weights = jnp.exp2(jnp.concatenate([first, rest], axis=1) - most_score)
                part_ref[member] = 1.0 / jnp.sum(weights, axis=1, keepdims=True)
                total_ref[member] = lax.dot_general(
                    weights.astype(jnp.bfloat16),
                    near[member * NBLK + b, :total, :lat],
                    (((1,), (0,)), ((), ())),
                    preferred_element_type=jnp.float32,
                )

        ends = range(TILE, most + 1, TILE)
        needs = counts
        choices = list(itertools.product(ends, repeat=cpg))
        if len(choices) > MOST_BODIES:
            needs = [functools.reduce(jnp.maximum, counts)] * cpg
            choices = [(total,) * cpg for total in ends]
        for totals in choices:
            fits = functools.reduce(
                jnp.logical_and,
                [jnp.logical_and(n > total - TILE, n <= total) for n, total in zip(needs, totals)],
            )
            pl.when(fits)(functools.partial(attend, totals))

        @pl.when(b >= 1)
        def _():
            for member in range(cpg):
                out_copy(b - 1, member, slot).start()

        return 0

    lax.fori_loop(0, NBLK, step, 0)
    last = (NBLK + 1) % 2
    for member in range(cpg):
        out_copy(NBLK - 3, member, last).wait()
    put(last)
    for member in range(cpg):
        out_copy(NBLK - 1, member, last).start()
    for member in range(cpg):
        out_copy(NBLK - 2, member, 1 - last).wait()
        out_copy(NBLK - 1, member, last).wait()


def shards(queries, keys, block_mask, summary_start):
    row_total, head_count, key_width = queries.shape
    lat_width = key_width - ROPE
    seq_count = lax.axis_size("seq")
    total_cands = block_mask.shape[0]
    cpg = total_cands // seq_count
    seq_len = row_total // cpg
    block_len = seq_len // NBLK
    summ_len = block_len // 2
    most = NBLK * block_len + (total_cands - 1) * summ_len
    most = -(-most // TILE) * TILE
    vmem = pl.BlockSpec(memory_space=pltpu.VMEM)
    smem = pl.BlockSpec(memory_space=pltpu.SMEM)

    held, other, by_head = gather_steps(keys, queries)
    first, second = step_orders(lax.axis_size("exp"))
    own = pl.pallas_call(
        functools.partial(pick_kernel, cpg, (first, second)),
        out_shape=jax.ShapeDtypeStruct((cpg * summ_len, key_width), keys.dtype),
        in_specs=[vmem] * 5,
        out_specs=vmem,
        compiler_params=grant(2),
        name="pick",
    )(summary_start.reshape(1, -1), *held, *other)
    ordered = pl.pallas_call(
        functools.partial(order_kernel, slot_offsets(first), slot_offsets(second)),
        out_shape=jax.ShapeDtypeStruct((row_total, key_width), keys.dtype),
        in_specs=[vmem] * 4,
        out_specs=vmem,
        compiler_params=grant(2),
        cost_estimate=pl.CostEstimate(flops=10**9, bytes_accessed=0, transcendentals=0),
        name="order",
    )(*held, *other)
    dims = (head_count, cpg, total_cands, seq_len, block_len, summ_len, lat_width)
    near_rows = NBLK * block_len + (total_cands - 1) * summ_len + TILE
    near = pl.pallas_call(
        functools.partial(prepare_kernel, dims),
        out_shape=jax.ShapeDtypeStruct((cpg * NBLK, near_rows, key_width), keys.dtype),
        in_specs=[smem, vmem, vmem],
        out_specs=vmem,
        compiler_params=grant(2),
        cost_estimate=pl.CostEstimate(flops=10**9, bytes_accessed=0, transcendentals=0),
        name="prepare",
    )(block_mask, ordered, own)
    sums = own
    bit = 1
    while bit < seq_count:
        pairs = [(i, i ^ bit) for i in range(seq_count)]
        got = lax.ppermute(sums, "seq", pairs)
        if 2 * bit >= seq_count:
            got, near = lax.optimization_barrier((got, near))
        sums = join(sums, got)
        bit *= 2
    rows = head_count * block_len
    return pl.pallas_call(
        functools.partial(attend_kernel, dims, most),
        out_shape=[
            jax.ShapeDtypeStruct((row_total, head_count, lat_width), queries.dtype),
            jax.ShapeDtypeStruct(near.shape, near.dtype),
        ],
        in_specs=[smem, vmem, vmem] + [vmem] * len(by_head),
        out_specs=[pl.BlockSpec(memory_space=pl.ANY), vmem],
        scratch_shapes=[
            pltpu.VMEM((cpg, rows, lat_width), jnp.float32),
            pltpu.VMEM((cpg, rows, 1), jnp.float32),
            pltpu.VMEM((2, cpg, block_len, head_count, lat_width), queries.dtype),
            pltpu.SemaphoreType.DMA((2, cpg)),
        ],
        input_output_aliases={1: 1},
        compiler_params=grant(20),
        name="attend",
    )(block_mask, near, sums, *by_head)[0]


def solution(mesh):
    placed = (P("seq", "exp", None), P(("seq", "exp"), None), P(), P())
    return jax.shard_map(
        shards, mesh=mesh, in_specs=placed, out_specs=P("seq", "exp", None), check_vma=False
    )
```

profile of v0, /device:TPU:0, one launch (start us, length us, event | category | flops | bytes accessed | tf_op | source)
XLA Modules:
  0.0 37.4 jit_solution(9384397142807649234)
XLA Ops:
  0.0 4.1 %collective-permute-start = (bf16[1,64,576]{2,1,0:T(8,128)(2,1)}, bf16[1,64,576]{2,1,0:T(8,128)(2,1)S(1)}, u32[]{:S(2)}, u32[]{:S(2)}) collective-permute-start(bf16[1,64,576]{2,1,0:T(8,128)(2,1)} %bitcast.5), channel_id=1, source_target_pairs={{0,8},{1,5},{2,10},{3,7},{4,12},{5,1},{6,14},{7,3},{8,0},{9,13},{1... | collective-permute-start | bytes 221192 | tf_op jit(solution)/shard_map/ppermute | solution.py:104
  4.1 0.9 %copy-done.1 = bf16[64,576]{1,0:T(8,128)(2,1)S(1)} copy-done((bf16[64,576]{1,0:T(8,128)(2,1)S(1)}, bf16[64,576]{1,0:T(8,128)(2,1)}, u32[]{:S(2)}) %copy-start.1) | copy-done | bytes 73752
  5.0 1.7 %collective-permute-done.second_ref = bf16[1,64,576]{2,1,0:T(8,128)(2,1)S(1)} collective-permute-done((bf16[1,64,576]{2,1,0:T(8,128)(2,1)}, bf16[1,64,576]{2,1,0:T(8,128)(2,1)S(1)}, u32[]{:S(2)}, u32[]{:S(2)}) %collective-permute-start) | collective-permute-done | bytes 73760 | tf_op jit(solution)/shard_map/ppermute | solution.py:104
  6.7 1.9 %collective-permute-start.1 = (bf16[2,64,576]{2,1,0:T(8,128)(2,1)S(1)}, bf16[2,64,576]{2,1,0:T(8,128)(2,1)S(1)}, u32[]{:S(2)}, u32[]{:S(2)}) collective-permute-start(bf16[2,64,576]{2,1,0:T(8,128)(2,1)S(1)} %join.3.first_ref), channel_id=1, source_target_pairs={{0,2},{1,9},{2,0},{3,11},{4,6},{5,13},{6,4},{7,15},{8,10},{9,1},{1... | collective-permute-start | bytes 442376 | tf_op jit(solution)/shard_map/ppermute | solution.py:104
  8.6 2.3 %copy-done = bf16[1024,4,576]{0,2,1:T(8,128)(2,1)S(1)} copy-done((bf16[1024,4,576]{0,2,1:T(8,128)(2,1)S(1)}, bf16[1024,4,576]{0,2,1:T(8,128)(2,1)}, u32[]{:S(2)}) %copy-start) | copy-done | bytes 4718616
  11.0 0.8 %turn.2.refs_0_ = bf16[1,1024,576]{2,1,0:T(8,128)(2,1)S(1)} custom-call(bf16[4,576,1024]{2,1,0:T(8,128)(2,1)S(1)} %bitcast.3), custom_call_target="tpu_custom_call" | custom-call | tf_op jit(solution)/shard_map/turn/pallas_call | solution.py:81
  11.7 0.4 collective-permute-done.1.second_ref
  12.1 0.0 copy-start.3
  12.1 0.1 collective-permute-start.3
  12.2 2.1 %collective-permute-start.2 = (bf16[4,64,576]{2,1,0:T(8,128)(2,1)S(1)}, bf16[4,64,576]{2,1,0:T(8,128)(2,1)S(1)}, u32[]{:S(2)}, u32[]{:S(2)}) collective-permute-start(bf16[4,64,576]{2,1,0:T(8,128)(2,1)S(1)} %join.4.refs_0_), channel_id=1, source_target_pairs={{0,4},{1,3},{2,6},{3,1},{4,0},{5,7},{6,2},{7,5},{8,12},{9,11},{10,... | collective-permute-start | bytes 884744 | tf_op jit(solution)/shard_map/ppermute | solution.py:104
  14.3 2.3 %turn.3.refs_1_ = bf16[3,1024,576]{2,1,0:T(8,128)(2,1)S(1)} custom-call(bf16[4,576,1024]{2,1,0:T(8,128)(2,1)S(1)} %bitcast.4), custom_call_target="tpu_custom_call" | custom-call | tf_op jit(solution)/shard_map/turn/pallas_call | solution.py:81
  16.6 0.0 copy-start.2
  16.6 0.0 collective-permute-done.3.refs_2_
  16.6 2.7 %collective-permute-done.2.refs_1_ = bf16[4,64,576]{2,1,0:T(8,128)(2,1)S(1)} collective-permute-done((bf16[4,64,576]{2,1,0:T(8,128)(2,1)S(1)}, bf16[4,64,576]{2,1,0:T(8,128)(2,1)S(1)}, u32[]{:S(2)}, u32[]{:S(2)}) %collective-permute-start.2) | collective-permute-done | bytes 294944 | tf_op jit(solution)/shard_map/ppermute | solution.py:104
  19.4 0.0 collective-permute-start.4
  19.4 1.6 %collective-permute-done.4.refs_3_ = bf16[4,64,576]{2,1,0:T(8,128)(2,1)S(1)} collective-permute-done((bf16[4,64,576]{2,1,0:T(8,128)(2,1)S(1)}, bf16[4,64,576]{2,1,0:T(8,128)(2,1)S(1)}, u32[]{:S(2)}, u32[]{:S(2)}) %collective-permute-start.4) | collective-permute-done | bytes 294944 | tf_op jit(solution)/shard_map/ppermute | solution.py:118
  21.0 0.0 copy-done.3
  21.0 0.4 pick.1.own_ref.first_ref
  21.4 1.9 %collective-permute-start.5 = (bf16[128,576]{1,0:T(8,128)(2,1)S(1)}, bf16[128,576]{1,0:T(8,128)(2,1)S(1)}, u32[]{:S(2)}, u32[]{:S(2)}) collective-permute-start(bf16[128,576]{1,0:T(8,128)(2,1)S(1)} %pick.1.own_ref.first_ref), channel_id=1, source_target_pairs={{0,16},{16,0},{1,17},{17,1},{2,18},{18,2},{3,19},{19,3},{4,20},{20... | collective-permute-start | bytes 442376 | tf_op jit(solution)/shard_map/ppermute | solution.py:363
  23.3 0.1 order.1.keys_ref
  23.4 0.0 copy-done.2
  23.4 1.7 %prepare.1.got_ref = bf16[8,960,576]{2,1,0:T(8,128)(2,1)S(1)} custom-call(s32[4,4,8]{2,1,0:T(4,128)S(1)} %copy-done.2, bf16[1024,576]{1,0:T(8,128)(2,1)S(1)} %order.1.keys_ref, bf16[128,576]{1,0:T(8,128)(2,1)S(1)} %pick.1.own_ref.first_ref), custom_call_target="tpu_custom_call" | custom-call | flops 1000000000 | tf_op jit(solution)/shard_map/prepare/pallas_call | solution.py:350
  25.1 2.7 %collective-permute-done.5.second_ref = bf16[128,576]{1,0:T(8,128)(2,1)S(1)} collective-permute-done((bf16[128,576]{1,0:T(8,128)(2,1)S(1)}, bf16[128,576]{1,0:T(8,128)(2,1)S(1)}, u32[]{:S(2)}, u32[]{:S(2)}) %collective-permute-start.5) | collective-permute-done | bytes 147488 | tf_op jit(solution)/shard_map/ppermute | solution.py:363
  27.8 9.7 %attend.1 = (bf16[1024,4,512]{2,1,0:T(4,128)(2,1)}, bf16[8,960,576]{2,1,0:T(8,128)(2,1)S(1)}) custom-call(s32[4,4,8]{2,1,0:T(4,128)S(1)} %copy-done.2, bf16[8,960,576]{2,1,0:T(8,128)(2,1)S(1)} %prepare.1.got_ref, bf16[256,576]{1,0:T(8,128)(2,1)S(1)} %join.5.sums_ref, bf16[1,1024,576]{2,1,0:T(8,128)(2,1)S(1)} %turn.2.refs_0_, ...), custom_call_target="tpu_custom_call", output_to_operand_aliasing={{1}: (1, {})} | custom-call | tf_op jit(solution)/shard_map/attend/pallas_call | solution.py:369
  (6 shorter events, 0.1 us)
Async XLA Ops:
  0.0 6.7 %collective-permute-start = (bf16[1,64,576]{2,1,0:T(8,128)(2,1)}, bf16[1,64,576]{2,1,0:T(8,128)(2,1)S(1)}, u32[]{:S(2)}, u32[]{:S(2)}) collective-permute-start(bf16[1,64,576]{2,1,0:T(8,128)(2,1)} %bitcast.5), channel_id=1, source_target_pairs={{0,8},{1,5},{2,10},{3,7},{4,12},{5,1},{6,14},{7,3},{8,0},{9,13},{1... | collective-permute-start | bytes 221192 | tf_op jit(solution)/shard_map/ppermute | solution.py:104
  4.1 0.9 %copy-start.1 = (bf16[64,576]{1,0:T(8,128)(2,1)S(1)}, bf16[64,576]{1,0:T(8,128)(2,1)}, u32[]{:S(2)}) copy-start(bf16[64,576]{1,0:T(8,128)(2,1)} %param.5) | copy-start | bytes 221188
  6.7 5.4 %collective-permute-start.1 = (bf16[2,64,576]{2,1,0:T(8,128)(2,1)S(1)}, bf16[2,64,576]{2,1,0:T(8,128)(2,1)S(1)}, u32[]{:S(2)}, u32[]{:S(2)}) collective-permute-start(bf16[2,64,576]{2,1,0:T(8,128)(2,1)S(1)} %join.3.first_ref), channel_id=1, source_target_pairs={{0,2},{1,9},{2,0},{3,11},{4,6},{5,13},{6,4},{7,15},{8,10},{9,1},{1... | collective-permute-start | bytes 442376 | tf_op jit(solution)/shard_map/ppermute | solution.py:104
  8.6 2.3 %copy-start = (bf16[1024,4,576]{0,2,1:T(8,128)(2,1)S(1)}, bf16[1024,4,576]{0,2,1:T(8,128)(2,1)}, u32[]{:S(2)}) copy-start(bf16[1024,4,576]{0,2,1:T(8,128)(2,1)} %param.4) | copy-start | bytes 14155780
  12.1 8.9 %copy-start.3 = (s32[4]{0:T(128)S(1)}, s32[4]{0:T(128)}, u32[]{:S(2)}) copy-start(s32[4]{0:T(128)} %param.7) | copy-start | bytes 52
  12.1 4.5 %collective-permute-start.3 = (bf16[4,64,576]{2,1,0:T(8,128)(2,1)S(1)}, bf16[4,64,576]{2,1,0:T(8,128)(2,1)S(1)}, u32[]{:S(2)}, u32[]{:S(2)}) collective-permute-start(bf16[4,64,576]{2,1,0:T(8,128)(2,1)S(1)} %join.4.refs_0_), channel_id=1, source_target_pairs={{0,1},{1,0},{2,3},{3,2},{4,5},{5,4},{6,7},{7,6},{8,9},{9,8},{10,11... | collective-permute-start | bytes 884744 | tf_op jit(solution)/shard_map/ppermute | solution.py:109
  12.2 7.1 %collective-permute-start.2 = (bf16[4,64,576]{2,1,0:T(8,128)(2,1)S(1)}, bf16[4,64,576]{2,1,0:T(8,128)(2,1)S(1)}, u32[]{:S(2)}, u32[]{:S(2)}) collective-permute-start(bf16[4,64,576]{2,1,0:T(8,128)(2,1)S(1)} %join.4.refs_0_), channel_id=1, source_target_pairs={{0,4},{1,3},{2,6},{3,1},{4,0},{5,7},{6,2},{7,5},{8,12},{9,11},{10,... | collective-permute-start | bytes 884744 | tf_op jit(solution)/shard_map/ppermute | solution.py:104
  16.6 6.8 %copy-start.2 = (s32[4,4,8]{2,1,0:T(4,128)S(1)}, s32[4,4,8]{2,1,0:T(4,128)}, u32[]{:S(2)}) copy-start(s32[4,4,8]{2,1,0:T(4,128)} %mask_ref.3) | copy-start | bytes 1540
  19.4 1.6 %collective-permute-start.4 = (bf16[4,64,576]{2,1,0:T(8,128)(2,1)S(1)}, bf16[4,64,576]{2,1,0:T(8,128)(2,1)S(1)}, u32[]{:S(2)}, u32[]{:S(2)}) collective-permute-start(bf16[4,64,576]{2,1,0:T(8,128)(2,1)S(1)} %collective-permute-done.2.refs_1_), channel_id=1, source_target_pairs={{0,1},{1,0},{2,3},{3,2},{4,5},{5,4},{6,7},{7,6},{8,9},{9,8},{10,11... | collective-permute-start | bytes 884744 | tf_op jit(solution)/shard_map/ppermute | solution.py:118
  21.4 6.4 %collective-permute-start.5 = (bf16[128,576]{1,0:T(8,128)(2,1)S(1)}, bf16[128,576]{1,0:T(8,128)(2,1)S(1)}, u32[]{:S(2)}, u32[]{:S(2)}) collective-permute-start(bf16[128,576]{1,0:T(8,128)(2,1)S(1)} %pick.1.own_ref.first_ref), channel_id=1, source_target_pairs={{0,16},{16,0},{1,17},{17,1},{2,18},{18,2},{3,19},{19,3},{4,20},{20... | collective-permute-start | bytes 442376 | tf_op jit(solution)/shard_map/ppermute | solution.py:363
where the time goes:
time: 38.1 us; the launch traced here: 37.4 us
  Pallas kernels  15 us (39%)
  starting transfers between devices  10 us (26%)
  waiting for transfers between devices  9.07 us (24%)
  local copies, waits for them, and re-layouts  3.27 us (9%)
    pallas_call x1, Pallas kernels, shards(): pl.pallas_call(functools.partial(attend_kernel, dims, most), out_shape=[j...  9.65 us
    ppermute x3, starting transfers between devices, gather_steps(): got = lax.ppermute(held, 'exp', pairs)  8.04 us
    ppermute x3, waiting for transfers between devices, gather_steps(): got = lax.ppermute(held, 'exp', pairs)  4.77 us
    unnamed x8, local copies, waits for them, and re-layouts  3.27 us
    pallas_call x2, Pallas kernels, turn(): pl.pallas_call(turn_kernel, out_shape=jax.ShapeDtypeStruct((total, rows,...  3.1 us
    ppermute x1, waiting for transfers between devices, shards(): got = lax.ppermute(sums, 'seq', pairs)  2.67 us
    ppermute x1, starting transfers between devices, shards(): got = lax.ppermute(sums, 'seq', pairs)  1.89 us
    pallas_call x1, Pallas kernels, shards(): pl.pallas_call(functools.partial(prepare_kernel, dims), out_shape=jax.Sha...  1.69 us
  transfers between devices with their start and end apart: 6, of which 5 were waited for; matrix products, arithmetic and copies ran while one was open for 0% of the time, Pallas kernels for 13%

commit v1 on v0

--- a/solution.py
+++ b/solution.py
@@ -147,6 +147,20 @@
                 @pl.when(buffer == number)
                 def _():
                     own_ref[at, :] = ref[lax.rem(slot, half), pl.ds(inside, piece), :]
+
+
+def half_kernel(own_ref, out_ref):
+    part = lax.axis_index("exp") % 2
+    summ = out_ref.shape[0]
+    out_ref[...] = own_ref[pl.ds(pl.multiple_of(part * summ, summ), summ), :]
+
+
+def both_kernel(own_ref, got_ref, rest_ref, out_ref):
+    part = lax.axis_index("exp") % 2
+    summ = got_ref.shape[0]
+    out_ref[: 2 * summ, :] = own_ref[...]
+    out_ref[pl.ds(pl.multiple_of((2 + part) * summ, summ), summ), :] = got_ref[...]
+    out_ref[pl.ds(pl.multiple_of((3 - part) * summ, summ), summ), :] = rest_ref[...]
 
 
 def order_kernel(offsets_a, offsets_b, *refs):
@@ -358,6 +372,28 @@
     )(block_mask, ordered, own)
     sums = own
     bit = 1
+    if seq_count == 2 and cpg == 2:
+        mine = pl.pallas_call(
+            half_kernel,
+            out_shape=jax.ShapeDtypeStruct((summ_len, key_width), keys.dtype),
+            in_specs=[vmem],
+            out_specs=vmem,
+            compiler_params=grant(2),
+            name="half",
+        )(own)
+        got = lax.ppermute(mine, "seq", [(0, 1), (1, 0)])
+        got, near = lax.optimization_barrier((got, near))
+        exp_count = lax.axis_size("exp")
+        rest = lax.ppermute(got, "exp", [(i, i ^ 1) for i in range(exp_count)])
+        sums = pl.pallas_call(
+            both_kernel,
+            out_shape=jax.ShapeDtypeStruct((4 * summ_len, key_width), keys.dtype),
+            in_specs=[vmem] * 3,
+            out_specs=vmem,
+            compiler_params=grant(2),
+            name="both",
+        )(own, got, rest)
+        bit = seq_count
     while bit < seq_count:
         pairs = [(i, i ^ bit) for i in range(seq_count)]
         got = lax.ppermute(sums, "seq", pairs)

time: 38.1 us -> 37.2 us (0.976)
  waiting for transfers between devices: 9.07 us -> 8.65 us
  Pallas kernels: 15 us -> 14.6 us
    ppermute x1 -> x2, waiting for transfers between devices: 2.67 us -> 2.25 us  [the longest x1 1.27 us: shards(): rest = lax.ppermute(got, 'exp', [(i, i ^ 1) for i in range(exp_count)])]
    ppermute x1 -> x2, starting transfers between devices: 1.89 us -> 1.89 us  [the longest x1 1.89 us: shards(): got = lax.ppermute(mine, 'seq', [(0, 1), (1, 0)])]
  transfers between devices with their start and end apart: 6 -> 7, of which waited for: 5 -> 6; matrix products, arithmetic and copies ran while one was open for 0% -> 0% of each run, Pallas kernels for 13% -> 13%
where the time goes in v1:
time: 37.2 us; the launch traced here: 36.6 us
  Pallas kernels  14.6 us (39%)
  starting transfers between devices  10 us (27%)
  waiting for transfers between devices  8.65 us (23%)
  local copies, waits for them, and re-layouts  3.27 us (9%)
    pallas_call x1, Pallas kernels, shards(): pl.pallas_call(functools.partial(attend_kernel, dims, most), out_shape=[j...  9.3 us
    ppermute x3, starting transfers between devices, gather_steps(): got = lax.ppermute(held, 'exp', pairs)  8.04 us
    ppermute x3, waiting for transfers between devices, gather_steps(): got = lax.ppermute(held, 'exp', pairs)  4.77 us
    unnamed x8, local copies, waits for them, and re-layouts  3.27 us
    pallas_call x2, Pallas kernels, turn(): pl.pallas_call(turn_kernel, out_shape=jax.ShapeDtypeStruct((total, rows,...  3.1 us
    ppermute x1, starting transfers between devices, shards(): got = lax.ppermute(mine, 'seq', [(0, 1), (1, 0)])  1.89 us
    pallas_call x1, Pallas kernels, shards(): pl.pallas_call(functools.partial(prepare_kernel, dims), out_shape=jax.Sha...  1.64 us
    ppermute x1, waiting for transfers between devices, gather_steps(): return ((held, got), (other, lax.ppermute(got, 'exp', swap)), by_head)  1.63 us
  transfers between devices with their start and end apart: 7, of which 6 were waited for; matrix products, arithmetic and copies ran while one was open for 0% of the time, Pallas kernels for 13%

profile of v1, /device:TPU:0, one launch (start us, length us, event | category | flops | bytes accessed | tf_op | source)
XLA Modules:
  0.0 36.6 jit_solution(682382339607353321)
XLA Ops:
  0.0 4.1 %collective-permute-start = (bf16[1,64,576]{2,1,0:T(8,128)(2,1)}, bf16[1,64,576]{2,1,0:T(8,128)(2,1)S(1)}, u32[]{:S(2)}, u32[]{:S(2)}) collective-permute-start(bf16[1,64,576]{2,1,0:T(8,128)(2,1)} %bitcast.5), channel_id=1, source_target_pairs={{0,8},{1,5},{2,10},{3,7},{4,12},{5,1},{6,14},{7,3},{8,0},{9,13},{1... | collective-permute-start | bytes 221192 | tf_op jit(solution)/shard_map/ppermute | solution.py:104
  4.1 0.9 %copy-done.1 = bf16[64,576]{1,0:T(8,128)(2,1)S(1)} copy-done((bf16[64,576]{1,0:T(8,128)(2,1)S(1)}, bf16[64,576]{1,0:T(8,128)(2,1)}, u32[]{:S(2)}) %copy-start.1) | copy-done | bytes 73752
  5.0 1.7 %collective-permute-done.second_ref = bf16[1,64,576]{2,1,0:T(8,128)(2,1)S(1)} collective-permute-done((bf16[1,64,576]{2,1,0:T(8,128)(2,1)}, bf16[1,64,576]{2,1,0:T(8,128)(2,1)S(1)}, u32[]{:S(2)}, u32[]{:S(2)}) %collective-permute-start) | collective-permute-done | bytes 73760 | tf_op jit(solution)/shard_map/ppermute | solution.py:104
  6.7 1.9 %collective-permute-start.1 = (bf16[2,64,576]{2,1,0:T(8,128)(2,1)S(1)}, bf16[2,64,576]{2,1,0:T(8,128)(2,1)S(1)}, u32[]{:S(2)}, u32[]{:S(2)}) collective-permute-start(bf16[2,64,576]{2,1,0:T(8,128)(2,1)S(1)} %join.2.first_ref), channel_id=1, source_target_pairs={{0,2},{1,9},{2,0},{3,11},{4,6},{5,13},{6,4},{7,15},{8,10},{9,1},{1... | collective-permute-start | bytes 442376 | tf_op jit(solution)/shard_map/ppermute | solution.py:104
  8.6 2.3 %copy-done = bf16[1024,4,576]{0,2,1:T(8,128)(2,1)S(1)} copy-done((bf16[1024,4,576]{0,2,1:T(8,128)(2,1)S(1)}, bf16[1024,4,576]{0,2,1:T(8,128)(2,1)}, u32[]{:S(2)}) %copy-start) | copy-done | bytes 4718616
  11.0 0.8 %turn.2.refs_0_ = bf16[1,1024,576]{2,1,0:T(8,128)(2,1)S(1)} custom-call(bf16[4,576,1024]{2,1,0:T(8,128)(2,1)S(1)} %bitcast.3), custom_call_target="tpu_custom_call" | custom-call | tf_op jit(solution)/shard_map/turn/pallas_call | solution.py:81
  11.7 0.4 collective-permute-done.1.second_ref
  12.1 0.0 copy-start.3
  12.1 0.1 collective-permute-start.3
  12.2 2.1 %collective-permute-start.2 = (bf16[4,64,576]{2,1,0:T(8,128)(2,1)S(1)}, bf16[4,64,576]{2,1,0:T(8,128)(2,1)S(1)}, u32[]{:S(2)}, u32[]{:S(2)}) collective-permute-start(bf16[4,64,576]{2,1,0:T(8,128)(2,1)S(1)} %join.3.refs_0_), channel_id=1, source_target_pairs={{0,4},{1,3},{2,6},{3,1},{4,0},{5,7},{6,2},{7,5},{8,12},{9,11},{10,... | collective-permute-start | bytes 884744 | tf_op jit(solution)/shard_map/ppermute | solution.py:104
  14.3 2.3 %turn.3.refs_1_ = bf16[3,1024,576]{2,1,0:T(8,128)(2,1)S(1)} custom-call(bf16[4,576,1024]{2,1,0:T(8,128)(2,1)S(1)} %bitcast.4), custom_call_target="tpu_custom_call" | custom-call | tf_op jit(solution)/shard_map/turn/pallas_call | solution.py:81
  16.6 0.0 copy-start.2
  16.6 0.0 collective-permute-done.3.refs_2_
  16.6 2.7 %collective-permute-done.2.refs_1_ = bf16[4,64,576]{2,1,0:T(8,128)(2,1)S(1)} collective-permute-done((bf16[4,64,576]{2,1,0:T(8,128)(2,1)S(1)}, bf16[4,64,576]{2,1,0:T(8,128)(2,1)S(1)}, u32[]{:S(2)}, u32[]{:S(2)}) %collective-permute-start.2) | collective-permute-done | bytes 294944 | tf_op jit(solution)/shard_map/ppermute | solution.py:104
  19.4 0.0 collective-permute-start.4
  19.4 1.6 %collective-permute-done.4.refs_3_ = bf16[4,64,576]{2,1,0:T(8,128)(2,1)S(1)} collective-permute-done((bf16[4,64,576]{2,1,0:T(8,128)(2,1)S(1)}, bf16[4,64,576]{2,1,0:T(8,128)(2,1)S(1)}, u32[]{:S(2)}, u32[]{:S(2)}) %collective-permute-start.4) | collective-permute-done | bytes 294944 | tf_op jit(solution)/shard_map/ppermute | solution.py:118
  21.0 0.4 pick.1.own_ref
  21.4 1.9 %collective-permute-start.5 = (bf16[64,576]{1,0:T(8,128)(2,1)S(1)}, bf16[64,576]{1,0:T(8,128)(2,1)S(1)}, u32[]{:S(2)}, u32[]{:S(2)}) collective-permute-start(bf16[64,576]{1,0:T(8,128)(2,1)S(1)} %half.1), channel_id=1, source_target_pairs={{0,16},{16,0},{1,17},{17,1},{2,18},{18,2},{3,19},{19,3},{4,20},{20... | collective-permute-start | bytes 221192 | tf_op jit(solution)/shard_map/ppermute | solution.py:384
  23.3 0.1 order.1.keys_ref
  23.4 1.6 %prepare.1.got_ref = bf16[8,960,576]{2,1,0:T(8,128)(2,1)S(1)} custom-call(s32[4,4,8]{2,1,0:T(4,128)S(1)} %copy-done.2, bf16[1024,576]{1,0:T(8,128)(2,1)S(1)} %order.1.keys_ref, bf16[128,576]{1,0:T(8,128)(2,1)S(1)} %pick.1.own_ref), custom_call_target="tpu_custom_call" | custom-call | flops 1000000000 | tf_op jit(solution)/shard_map/prepare/pallas_call | solution.py:364
  25.1 1.0 %collective-permute-done.5.got_ref = bf16[64,576]{1,0:T(8,128)(2,1)S(1)} collective-permute-done((bf16[64,576]{1,0:T(8,128)(2,1)S(1)}, bf16[64,576]{1,0:T(8,128)(2,1)S(1)}, u32[]{:S(2)}, u32[]{:S(2)}) %collective-permute-start.5) | collective-permute-done | bytes 73760 | tf_op jit(solution)/shard_map/ppermute | solution.py:384
  26.0 0.0 collective-permute-start.6
  26.0 1.3 %collective-permute-done.6.rest_ref = bf16[64,576]{1,0:T(8,128)(2,1)S(1)} collective-permute-done((bf16[64,576]{1,0:T(8,128)(2,1)S(1)}, bf16[64,576]{1,0:T(8,128)(2,1)S(1)}, u32[]{:S(2)}, u32[]{:S(2)}) %collective-permute-start.6) | collective-permute-done | bytes 73760 | tf_op jit(solution)/shard_map/ppermute | solution.py:387
  27.3 9.3 %attend.1 = (bf16[1024,4,512]{2,1,0:T(4,128)(2,1)}, bf16[8,960,576]{2,1,0:T(8,128)(2,1)S(1)}) custom-call(s32[4,4,8]{2,1,0:T(4,128)S(1)} %copy-done.2, bf16[8,960,576]{2,1,0:T(8,128)(2,1)S(1)} %prepare.1.got_ref, bf16[256,576]{1,0:T(8,128)(2,1)S(1)} %both.1.sums_ref, bf16[1,1024,576]{2,1,0:T(8,128)(2,1)S(1)} %turn.2.refs_0_, ...), custom_call_target="tpu_custom_call", output_to_operand_aliasing={{1}: (1, {})} | custom-call | tf_op jit(solution)/shard_map/attend/pallas_call | solution.py:405
  (9 shorter events, 0.1 us)
Async XLA Ops:
  0.0 6.7 %collective-permute-start = (bf16[1,64,576]{2,1,0:T(8,128)(2,1)}, bf16[1,64,576]{2,1,0:T(8,128)(2,1)S(1)}, u32[]{:S(2)}, u32[]{:S(2)}) collective-permute-start(bf16[1,64,576]{2,1,0:T(8,128)(2,1)} %bitcast.5), channel_id=1, source_target_pairs={{0,8},{1,5},{2,10},{3,7},{4,12},{5,1},{6,14},{7,3},{8,0},{9,13},{1... | collective-permute-start | bytes 221192 | tf_op jit(solution)/shard_map/ppermute | solution.py:104
  4.1 0.9 %copy-start.1 = (bf16[64,576]{1,0:T(8,128)(2,1)S(1)}, bf16[64,576]{1,0:T(8,128)(2,1)}, u32[]{:S(2)}) copy-start(bf16[64,576]{1,0:T(8,128)(2,1)} %param.5) | copy-start | bytes 221188
  6.7 5.4 %collective-permute-start.1 = (bf16[2,64,576]{2,1,0:T(8,128)(2,1)S(1)}, bf16[2,64,576]{2,1,0:T(8,128)(2,1)S(1)}, u32[]{:S(2)}, u32[]{:S(2)}) collective-permute-start(bf16[2,64,576]{2,1,0:T(8,128)(2,1)S(1)} %join.2.first_ref), channel_id=1, source_target_pairs={{0,2},{1,9},{2,0},{3,11},{4,6},{5,13},{6,4},{7,15},{8,10},{9,1},{1... | collective-permute-start | bytes 442376 | tf_op jit(solution)/shard_map/ppermute | solution.py:104
  8.6 2.3 %copy-start = (bf16[1024,4,576]{0,2,1:T(8,128)(2,1)S(1)}, bf16[1024,4,576]{0,2,1:T(8,128)(2,1)}, u32[]{:S(2)}) copy-start(bf16[1024,4,576]{0,2,1:T(8,128)(2,1)} %param.4) | copy-start | bytes 14155780
  12.1 8.9 %copy-start.3 = (s32[4]{0:T(128)S(1)}, s32[4]{0:T(128)}, u32[]{:S(2)}) copy-start(s32[4]{0:T(128)} %param.7) | copy-start | bytes 52
  12.1 4.5 %collective-permute-start.3 = (bf16[4,64,576]{2,1,0:T(8,128)(2,1)S(1)}, bf16[4,64,576]{2,1,0:T(8,128)(2,1)S(1)}, u32[]{:S(2)}, u32[]{:S(2)}) collective-permute-start(bf16[4,64,576]{2,1,0:T(8,128)(2,1)S(1)} %join.3.refs_0_), channel_id=1, source_target_pairs={{0,1},{1,0},{2,3},{3,2},{4,5},{5,4},{6,7},{7,6},{8,9},{9,8},{10,11... | collective-permute-start | bytes 884744 | tf_op jit(solution)/shard_map/ppermute | solution.py:109
  12.2 7.1 %collective-permute-start.2 = (bf16[4,64,576]{2,1,0:T(8,128)(2,1)S(1)}, bf16[4,64,576]{2,1,0:T(8,128)(2,1)S(1)}, u32[]{:S(2)}, u32[]{:S(2)}) collective-permute-start(bf16[4,64,576]{2,1,0:T(8,128)(2,1)S(1)} %join.3.refs_0_), channel_id=1, source_target_pairs={{0,4},{1,3},{2,6},{3,1},{4,0},{5,7},{6,2},{7,5},{8,12},{9,11},{10,... | collective-permute-start | bytes 884744 | tf_op jit(solution)/shard_map/ppermute | solution.py:104
  16.6 6.8 %copy-start.2 = (s32[4,4,8]{2,1,0:T(4,128)S(1)}, s32[4,4,8]{2,1,0:T(4,128)}, u32[]{:S(2)}) copy-start(s32[4,4,8]{2,1,0:T(4,128)} %mask_ref.3) | copy-start | bytes 1540
  19.4 1.6 %collective-permute-start.4 = (bf16[4,64,576]{2,1,0:T(8,128)(2,1)S(1)}, bf16[4,64,576]{2,1,0:T(8,128)(2,1)S(1)}, u32[]{:S(2)}, u32[]{:S(2)}) collective-permute-start(bf16[4,64,576]{2,1,0:T(8,128)(2,1)S(1)} %collective-permute-done.2.refs_1_), channel_id=1, source_target_pairs={{0,1},{1,0},{2,3},{3,2},{4,5},{5,4},{6,7},{7,6},{8,9},{9,8},{10,11... | collective-permute-start | bytes 884744 | tf_op jit(solution)/shard_map/ppermute | solution.py:118
  21.4 4.6 %collective-permute-start.5 = (bf16[64,576]{1,0:T(8,128)(2,1)S(1)}, bf16[64,576]{1,0:T(8,128)(2,1)S(1)}, u32[]{:S(2)}, u32[]{:S(2)}) collective-permute-start(bf16[64,576]{1,0:T(8,128)(2,1)S(1)} %half.1), channel_id=1, source_target_pairs={{0,16},{16,0},{1,17},{17,1},{2,18},{18,2},{3,19},{19,3},{4,20},{20... | collective-permute-start | bytes 221192 | tf_op jit(solution)/shard_map/ppermute | solution.py:384
  26.0 1.3 %collective-permute-start.6 = (bf16[64,576]{1,0:T(8,128)(2,1)S(1)}, bf16[64,576]{1,0:T(8,128)(2,1)S(1)}, u32[]{:S(2)}, u32[]{:S(2)}) collective-permute-start(bf16[64,576]{1,0:T(8,128)(2,1)S(1)} %collective-permute-done.5.got_ref), channel_id=1, source_target_pairs={{0,1},{1,0},{2,3},{3,2},{4,5},{5,4},{6,7},{7,6},{8,9},{9,8},{10,11... | collective-permute-start | bytes 221192 | tf_op jit(solution)/shard_map/ppermute | solution.py:387
